TPU v7x, 256 devices: a whole 4x4x8 slice. The times are simulated.
256 devices in a mesh: grid: 64 (over x_lo, y, z), tm: 4 (over x_hi, core).
Axes of the slice: x: 4 (x_hi: 2, x_lo: 2; x = x_hi * 2 + x_lo), y: 4, z: 8, core: 2. Of those that a mesh axis runs over, the one named last changes fastest.
Arguments:
- temps: float32 [2048, 262144], P('tm', 'grid'), may hold values from -6 to 12
- area_weight: float32 [262144], P('grid'), may hold values from 0.3 to 1
- eofs: bfloat16 [262144, 256], P('grid'), may hold values from -0.03125 to 0.03125
Outputs:
- lag_tiles: float32 [32, 256, 256], P('tm', 'grid')
All inputs are finite; a program needn't handle non-finite values.
Results may differ from a plain program's by a relative error of at most 0.0003.
Values sent between devices are 32-bit elements; how exact they have to be, the bound alone decides.
No kernel may reach another device: no remote copies, remote signals or barrier semaphores. Data moves between devices by JAX's collectives and lax.ppermute only.
A program may use at most 64 MiB of HBM per device.

v0:
```python
import jax
import jax.numpy as jnp
from jax import lax
from jax.sharding import PartitionSpec as P

LAGS = 32


def lagged_columns(own_block, total_rows, first_lag, lag_count):
    empty = jnp.zeros((total_rows, own_block.shape[1]), jnp.float32)
    pieces = [
        lax.dynamic_update_slice_in_dim(empty, own_block, first_lag + offset, 0)
        for offset in range(lag_count)
    ]
    return jnp.concatenate(pieces, axis=1)


def tile_product(own_block, extended, first_lag, lag_count):
    shifted = lagged_columns(own_block, extended.shape[0], first_lag, lag_count)
    product = jnp.einsum("sm,sh->mh", shifted, extended, precision=lax.Precision.HIGHEST)
    return product.reshape(lag_count, own_block.shape[1], extended.shape[1])


def shards(temps, area_weight, eofs):
    hours_dev = temps.shape[0]
    hour_count = hours_dev * lax.axis_size("tm")
    column_sums = lax.psum(jnp.sum(temps, axis=0), "tm")
    column_mean = column_sums / hour_count
    anomaly = ((temps - column_mean) * area_weight).astype(jnp.bfloat16)
    partial_sums = jnp.dot(anomaly, eofs, preferred_element_type=jnp.float32)
    components = lax.psum(partial_sums, "grid")
    channels = components.shape[1]
    chan_block = channels // lax.axis_size("grid")
    chan_start = lax.axis_index("grid") * chan_block
    all_rows = lax.all_gather(components, "tm", axis=0, tiled=True)
    own_block = lax.dynamic_slice_in_dim(all_rows, chan_start, chan_block, 1)
    extended = jnp.concatenate([all_rows, jnp.zeros((LAGS - 1, channels), jnp.float32)], axis=0)
    lag_count = LAGS // lax.axis_size("tm")
    first_lag = lax.axis_index("tm") * lag_count
    lag_tiles = tile_product(own_block, extended, first_lag, lag_count)
    return lag_tiles / hour_count


def solution(mesh):
    placed = (P("tm", "grid"), P("grid"), P("grid", None))
    return jax.shard_map(
        shards, mesh=mesh, in_specs=placed, out_specs=P("tm", "grid", None), check_vma=False
    )
```

profile of v0, /device:TPU:1, one launch (start us, length us, event | category | flops | bytes accessed | tf_op | source)
XLA Modules:
  0.0 680.8 jit_solution(3333425734207268882)
XLA Ops:
  6.5 0.0 copy-start
  6.5 0.0 copy-start.1
  6.5 0.0 all-reduce.3.cloned.1.call-start
  6.5 3.9 reduce_sum.9
  10.5 13.5 %psum.14 = f32[4096]{0:T(1024)S(1)} all-reduce(f32[4096]{0:T(1024)S(1)} %reduce_sum.9), channel_id=1, replica_groups=mesh['grid'=64,'tm'=4] {'tm'}, use_global_device_ids=true, to_apply=%region_1.0 | all-reduce | flops 4096 | bytes 32768 | tf_op jit(solution)/shard_map/psum | solution.py:27
  24.0 0.0 copy-done
  24.0 0.0 copy-done.1
  24.0 5.4 fusion
  29.4 0.0 all-reduce.3.cloned.1.call-update
  29.4 0.0 all-gather.2.cloned.1.call-start
  29.5 561.3 %all-reduce.3.cloned.1.call-done = f32[512,256]{1,0:T(8,128)} async-done(((f32[512,256]{1,0:T(8,128)}), f32[512,256]{1,0:T(8,128)}) %all-reduce.3.cloned.1.call-update) | async-done | bytes 524304 | tf_op jit(solution)/shard_map/psum | solution.py:31
  590.7 0.0 all-gather.2.cloned.1.call-update
  590.8 73.3 %all-gather.2.cloned.1.call-done = f32[2048,256]{1,0:T(8,128)} async-done(((f32[512,256]{1,0:T(8,128)}), f32[2048,256]{1,0:T(8,128)}) %all-gather.2.cloned.1.call-update) | async-done | bytes 2097168 | tf_op jit(solution)/shard_map/all_gather | solution.py:35
  664.0 1.6 constant_dynamic-slice_fusion
  665.6 0.3 copy.4
  666.0 0.5 dynamic_update_slice.25
  666.5 0.5 dynamic_update_slice.26
  667.1 0.5 dynamic_update_slice.27
  667.7 0.5 dynamic_update_slice.28
  668.2 0.5 dynamic_update_slice.29
  668.8 0.5 dynamic_update_slice.30
  669.4 0.5 dynamic_update_slice.31
  669.9 0.5 dynamic_update_slice.24
  670.5 0.2 concatenate.6
  670.6 2.7 fusion.5
  673.3 0.6 div.18
  (9 shorter events, 0.1 us)
Async XLA Ops:
  6.5 17.4 %copy-start = (bf16[4096,256]{1,0:T(8,128)(2,1)S(1)}, bf16[4096,256]{1,0:T(8,128)(2,1)}, u32[]{:S(2)}) copy-start(bf16[4096,256]{1,0:T(8,128)(2,1)} %param.5) | copy-start | bytes 6291460
  6.5 17.4 %copy-start.1 = (f32[4096]{0:T(1024)S(1)}, f32[4096]{0:T(1024)}, u32[]{:S(2)}) copy-start(f32[4096]{0:T(1024)} %param.4) | copy-start | bytes 49156
  6.5 584.2 %all-reduce.3.cloned.1.call-start = ((), (), s32[]{:S(2)}) async-start(), calls=%async_computation | async-start | bytes 1048576 | tf_op jit(solution)/shard_map/psum | solution.py:31
  29.4 634.6 %all-gather.2.cloned.1.call-start = ((), (), s32[]{:S(2)}) async-start(), calls=%async_computation.1 | async-start | bytes 2621440 | tf_op jit(solution)/shard_map/all_gather | solution.py:35
Sparse Core Ops, SparseCore 0:
  29.5 561.1 all-reduce.2
  592.7 71.3 all-gather.1
where the time goes:
time: 681 us
  waiting for transfers between devices  635 us (93%)
  between operations  13.6 us (2%)
  blocking collectives  13.5 us (2%)
  matrix products  8.09 us (1%)
  local copies, waits for them, and re-layouts  7.09 us (1%)
    psum x1, waiting for transfers between devices, shards(): components = lax.psum(partial_sums, 'grid')  561 us
    all_gather x1, waiting for transfers between devices, shards(): all_rows = lax.all_gather(components, 'tm', axis=0, tiled=True)  73.3 us
  transfers between devices with their start and end apart: 2, of which 2 were waited for; matrix products, arithmetic and copies ran while one was open for 0% of the time, Pallas kernels for 0%

commit v1 on v0

--- a/solution.py
+++ b/solution.py
@@ -28,7 +28,7 @@
     column_mean = column_sums / hour_count
     anomaly = ((temps - column_mean) * area_weight).astype(jnp.bfloat16)
     partial_sums = jnp.dot(anomaly, eofs, preferred_element_type=jnp.float32)
-    components = lax.psum(partial_sums, "grid")
+    components = jnp.sum(lax.all_gather(partial_sums, "grid"), axis=0)
     channels = components.shape[1]
     chan_block = channels // lax.axis_size("grid")
     chan_start = lax.axis_index("grid") * chan_block

time: 681 us -> 468 us (0.69)
  waiting for transfers between devices: 635 us -> 409 us
  other arithmetic: 3.94 us -> 16.6 us
    psum x1 -> x0, waiting for transfers between devices: 561 us -> none  [shards(): components = lax.psum(partial_sums, 'grid')]
    all_gather x0 -> x1, waiting for transfers between devices: none -> 375 us  [shards(): components = jnp.sum(lax.all_gather(partial_sums, 'grid'), axis=0)]
    all_gather x1, waiting for transfers between devices: 73.3 us -> 33.4 us  [shards(): all_rows = lax.all_gather(components, 'tm', axis=0, tiled=True)]
    reduce_sum x0 -> x1, other arithmetic: none -> 12.7 us  [shards(): components = jnp.sum(lax.all_gather(partial_sums, 'grid'), axis=0)]
where the time goes in v1:
time: 468 us
  waiting for transfers between devices  409 us (87%)
  other arithmetic  16.6 us (4%)
  between operations  13.6 us (3%)
  blocking collectives  13.5 us (3%)
  matrix products  8.1 us (2%)
  local copies, waits for them, and re-layouts  7.09 us (2%)
    all_gather x1, waiting for transfers between devices, shards(): components = jnp.sum(lax.all_gather(partial_sums, 'grid'), axis=0)  375 us
    all_gather x1, waiting for transfers between devices, shards(): all_rows = lax.all_gather(components, 'tm', axis=0, tiled=True)  33.4 us
    psum x1, blocking collectives, shards(): column_sums = lax.psum(jnp.sum(temps, axis=0), 'tm')  13.5 us
    reduce_sum x1, other arithmetic, shards(): components = jnp.sum(lax.all_gather(partial_sums, 'grid'), axis=0)  12.7 us
  transfers between devices with their start and end apart: 2, of which 2 were waited for; matrix products, arithmetic and copies ran while one was open for 0% of the time, Pallas kernels for 0%

profile of v1, /device:TPU:1, one launch (start us, length us, event | category | flops | bytes accessed | tf_op | source)
XLA Modules:
  0.0 467.7 jit_solution(11292719505856004789)
XLA Ops:
  6.5 0.0 copy-start
  6.5 0.0 copy-start.1
  6.5 0.0 all-gather.6.cloned.1.call-start
  6.5 3.9 reduce_sum.18
  10.5 13.5 %psum.7 = f32[4096]{0:T(1024)S(1)} all-reduce(f32[4096]{0:T(1024)S(1)} %reduce_sum.18), channel_id=1, replica_groups=mesh['grid'=64,'tm'=4] {'tm'}, use_global_device_ids=true, to_apply=%region_1.0 | all-reduce | flops 4096 | bytes 32768 | tf_op jit(solution)/shard_map/psum | solution.py:27
  24.0 0.0 copy-done
  24.0 0.0 copy-done.1
  24.0 5.4 %fusion = f32[512,256]{1,0:T(8,128)} fusion(bf16[4096,256]{1,0:T(8,128)(2,1)S(1)} %copy-done, f32[512,4096]{1,0:T(8,128)} %param.3, f32[4096]{0:T(1024)S(1)} %copy-done.1, f32[4096]{0:T(1024)S(1)} %broadcast_multiply_fusion), kind=kOutput, calls=%fused_computation.1 | convolution fusion | flops 1080033280 | bytes 11042816 | tf_op jit(solution)/shard_map/dot_general | solution.py:30
  29.4 0.0 all-gather.6.cloned.1.call-update
  29.4 0.0 all-gather.4.cloned.1.call-start
  29.5 375.5 %all-gather.6.cloned.1.call-done = f32[32768,256]{1,0:T(8,128)} async-done(((f32[512,256]{1,0:T(8,128)}), f32[32768,256]{1,0:T(8,128)}) %all-gather.6.cloned.1.call-update) | async-done | bytes 33554448 | tf_op jit(solution)/shard_map/all_gather | solution.py:31
  405.0 12.7 %reduce_sum.19 = f32[512,256]{1,0:T(8,128)} reduce(f32[64,512,256]{2,1,0:T(8,128)} %bitcast.3, f32[]{:T(128)} %constant.12.clone.1), dimensions={0}, to_apply=%region_2.0 | reduce | flops 8257536 | bytes 34078724 | tf_op jit(solution)/shard_map/reduce_sum | solution.py:31
  417.6 0.0 all-gather.4.cloned.1.call-update
  417.7 33.4 %all-gather.4.cloned.1.call-done = f32[2048,256]{1,0:T(8,128)} async-done(((f32[512,256]{1,0:T(8,128)}), f32[2048,256]{1,0:T(8,128)}) %all-gather.4.cloned.1.call-update) | async-done | bytes 2097168 | tf_op jit(solution)/shard_map/all_gather | solution.py:35
  451.0 1.6 constant_dynamic-slice_fusion
  452.6 0.3 copy.4
  452.9 0.5 dynamic_update_slice.25
  453.5 0.5 dynamic_update_slice.26
  454.1 0.5 dynamic_update_slice.27
  454.6 0.5 dynamic_update_slice.28
  455.2 0.5 dynamic_update_slice.29
  455.8 0.5 dynamic_update_slice.30
  456.3 0.5 dynamic_update_slice.31
  456.9 0.5 dynamic_update_slice.24
  457.5 0.2 concatenate.6
  457.6 2.7 fusion.5
  460.3 0.6 div.18
  (9 shorter events, 0.1 us)
Async XLA Ops:
  6.5 17.4 %copy-start = (bf16[4096,256]{1,0:T(8,128)(2,1)S(1)}, bf16[4096,256]{1,0:T(8,128)(2,1)}, u32[]{:S(2)}) copy-start(bf16[4096,256]{1,0:T(8,128)(2,1)} %param.5) | copy-start | bytes 6291460
  6.5 17.4 %copy-start.1 = (f32[4096]{0:T(1024)S(1)}, f32[4096]{0:T(1024)}, u32[]{:S(2)}) copy-start(f32[4096]{0:T(1024)} %param.4) | copy-start | bytes 49156
  6.5 398.4 %all-gather.6.cloned.1.call-start = ((), (), s32[]{:S(2)}) async-start(), calls=%async_computation.1 | async-start | bytes 34078720 | tf_op jit(solution)/shard_map/all_gather | solution.py:31
  29.4 421.6 %all-gather.4.cloned.1.call-start = ((), (), s32[]{:S(2)}) async-start(), calls=%async_computation | async-start | bytes 2621440 | tf_op jit(solution)/shard_map/all_gather | solution.py:35
Sparse Core Ops, SparseCore 0:
  29.6 375.3 all-gather.5
  417.8 33.1 all-gather.3
